TPU v7x, 32 devices: a whole 2x2x4 slice. The times are simulated.
32 devices in a mesh: group: 4 (over z), shard: 8 (over y, x, core).
Axes of the slice: x: 2, y: 2, z: 4, core: 2. Of those that a mesh axis runs over, the one named last changes fastest.
Arguments:
- query_hidden: bfloat16 [32, 32, 768], P(('group', 'shard')), may hold values from -6 to 6
- positive_hidden: bfloat16 [32, 64, 768], P(('group', 'shard')), may hold values from -6 to 6
- passage_store: bfloat16 [256, 64, 768], P('shard'), may hold values from -6 to 6
- negative_ids: int32 [32, 8], P(('group', 'shard')), may hold values from 0 to 255, as said below
- teacher_margins: int32 [32, 8], P(('group', 'shard')), may hold values from -4096 to 4095
- transform_weight: bfloat16 [768, 768], replicated, may hold values from -0.21875 to 0.21875
- vocab_weight: bfloat16 [768, 15360], P(None, 'shard'), may hold values from -0.21875 to 0.21875
- dense_weight: bfloat16 [768, 768], replicated, may hold values from -0.21875 to 0.21875
Outputs:
- student_margin: float32 [32, 8], P(('group', 'shard'))
- dense_grad: float32 [768, 768], replicated
Inputs may be any that keep to these rules, and one draw needn't show every extreme that they name: `negative_ids`: passage p is held by shard index p // 32. Among the 8 negatives of one index of group and shard, every store index is named by none or exactly 2 of them; one store index, drawn from the seed, is named 2 times by every index of group and shard.
All inputs are finite; a program needn't handle non-finite values.
Results may differ from a plain program's by a relative error of at most 0.0029.
Values may be sent and summed in bfloat16 or wider, within the bound.
A program may use at most 128 MiB of HBM per device.

v0:
```python
from functools import partial
import math
import jax
import jax.numpy as jnp
from jax import lax
from jax.sharding import PartitionSpec as P

CAP = 2


def encode(hidden, transform_weight):
    mixed_rows = jnp.dot(hidden, transform_weight, preferred_element_type=jnp.float32)
    active = jax.nn.gelu(mixed_rows, approximate=False)
    centre = jnp.mean(active, axis=-1, keepdims=True)
    spread = jnp.mean(jnp.square(active - centre), axis=-1, keepdims=True)
    return ((active - centre) * lax.rsqrt(spread + 1e-05)).astype(jnp.bfloat16)


def pool_single(sequence, vocab_weight):
    logits = jnp.dot(sequence, vocab_weight, preferred_element_type=jnp.float32)
    return jnp.max(jnp.log1p(jnp.maximum(logits, 0.0)), axis=0)


def pool_sequences(block_rows, offset, vocab_weight):
    return lax.map(partial(pool_single, vocab_weight=vocab_weight), block_rows, batch_size=8)


def add_outer(running, pieces):
    return running + jnp.einsum("rd,re->de", pieces[0], pieces[1], precision=lax.Precision.HIGHEST)


def body(
    query_hidden,
    positive_hidden,
    passage_store,
    negative_ids,
    teacher_margins,
    transform_weight,
    vocab_weight,
    dense_weight,
):
    shards = lax.axis_size("shard")
    queries_dev, negatives = negative_ids.shape
    store_rows, length, width = passage_store.shape
    vocab_total = vocab_weight.shape[1] * shards
    pooler = partial(pool_sequences, vocab_weight=vocab_weight)
    query_coded = encode(query_hidden, transform_weight)
    positive_coded = encode(positive_hidden, transform_weight)
    query_pool = pooler(lax.all_gather(query_coded, "shard", axis=0, tiled=True), jnp.int32(0))
    neg_total = queries_dev * negatives
    flat_ids = negative_ids.reshape(neg_total)
    owner_of = flat_ids // store_rows
    local_row = flat_ids % store_rows
    shard_ids = jnp.arange(shards, dtype=jnp.int32)
    owner_hit = (owner_of[:, None] == shard_ids[None, :]).astype(jnp.int32)
    earlier = jnp.cumsum(owner_hit, axis=0) - owner_hit
    slot_rank = jnp.sum(earlier * owner_hit, axis=1)
    slot_ids = jnp.arange(CAP, dtype=jnp.int32)
    slot_hit = (owner_hit[:, :, None] > 0) & (slot_rank[:, None, None] == slot_ids[None, None, :])
    asked_rows = jnp.sum(jnp.where(slot_hit, local_row[:, None, None], 0), axis=0)
    requests = jnp.where(jnp.any(slot_hit, axis=0), asked_rows, -1)
    asked_for = lax.all_to_all(requests, "shard", split_axis=0, concat_axis=0, tiled=True)
    is_valid = asked_for >= 0
    served = passage_store[jnp.clip(asked_for, 0, store_rows - 1)]
    served = jnp.where(is_valid[:, :, None, None], served, jnp.zeros((), served.dtype))
    fetched = lax.all_to_all(served, "shard", split_axis=0, concat_axis=0, tiled=True)
    negative_hidden = fetched.reshape(shards * CAP, length, width)[owner_of * CAP + slot_rank]
    negative_coded = encode(negative_hidden, transform_weight)
    passages = jnp.concatenate(
        [positive_coded[:, None], negative_coded.reshape(queries_dev, negatives, length, width)],
        axis=1,
    )
    passages = passages.reshape(queries_dev * (1 + negatives), length, width)
    passage_pool = pooler(lax.all_gather(passages, "shard", axis=0, tiled=True), jnp.int32(0))
    passage_pool = passage_pool.reshape(shards * queries_dev, 1 + negatives, -1)
    pair_terms = jnp.einsum("qv,qjv->qj", query_pool, passage_pool, precision=lax.Precision.HIGHEST)
    sparse = lax.psum_scatter(pair_terms, "shard", scatter_dimension=0, tiled=True) / math.sqrt(
        vocab_total
    )
    inv_root = 1.0 / math.sqrt(width)
    query_cls = query_hidden[:, 0, :]
    positive_cls = positive_hidden[:, 0, :]
    negative_cls = negative_hidden[:, 0, :].reshape(queries_dev, negatives, width)
    query_vec = jnp.dot(query_cls, dense_weight, preferred_element_type=jnp.float32)
    positive_vec = jnp.dot(positive_cls, dense_weight, preferred_element_type=jnp.float32)
    negative_vec = jnp.dot(negative_cls, dense_weight, preferred_element_type=jnp.float32)
    dense_pos = jnp.sum(query_vec * positive_vec, axis=1) * inv_root
    dense_neg = (
        jnp.einsum("qd,qkd->qk", query_vec, negative_vec, precision=lax.Precision.HIGHEST)
        * inv_root
    )
    pos_score = sparse[:, 0] + dense_pos
    neg_score = sparse[:, 1:] + dense_neg
    margin = pos_score[:, None] - neg_score
    target = teacher_margins.astype(jnp.float32) / 1024.0
    coef = (margin - target) / negatives
    coef_total = jnp.sum(coef, axis=1)
    grad_query = (
        coef_total[:, None] * positive_vec
        - jnp.einsum("qk,qkd->qd", coef, negative_vec, precision=lax.Precision.HIGHEST)
    ) * inv_root
    grad_positive = coef_total[:, None] * query_vec * inv_root
    grad_negative = -coef[:, :, None] * query_vec[:, None, :] * inv_root
    states = jnp.concatenate(
        [query_cls, positive_cls, negative_cls.reshape(-1, width)], axis=0
    ).astype(jnp.float32)
    factors = jnp.concatenate([grad_query, grad_positive, grad_negative.reshape(-1, width)], axis=0)
    empty = jnp.zeros((width, width), jnp.float32)
    dense_grad = add_outer(
        empty,
        (
            lax.all_gather(states, ("group", "shard"), axis=0, tiled=True),
            lax.all_gather(factors, ("group", "shard"), axis=0, tiled=True),
        ),
    )
    return (margin, dense_grad)


def solution(mesh):
    in_specs = (
        P(("group", "shard"), None, None),
        P(("group", "shard"), None, None),
        P("shard", None, None),
        P(("group", "shard"), None),
        P(("group", "shard"), None),
        P(),
        P(None, "shard"),
        P(),
    )
    out_specs = (P(("group", "shard"), None), P())
    return jax.shard_map(body, mesh=mesh, in_specs=in_specs, out_specs=out_specs, check_vma=False)
```

profile of v0, /device:TPU:0, one launch (start us, length us, event | category | flops | bytes accessed | tf_op | source)
XLA Modules:
  0.0 263.6 jit_solution(15380211158896153419)
XLA Ops:
  7.2 0.8 and_select_fusion.2
  8.6 9.7 %all_to_all.11 = s32[8,1,2]{2,1,0:T(1,128)S(1)} all-to-all(s32[8,1,2]{2,1,0:T(1,128)S(1)} %copy.29), channel_id=1, replica_groups=mesh['group'=4,'shard'=8] {'shard'}, dimensions={0} | all-to-all | bytes 128 | tf_op jit(solution)/shard_map/all_to_all | solution.py:62
  18.6 1.8 gather_fusion
  20.4 2.7 %broadcast_select_fusion = bf16[8,2,64,768]{3,2,1,0:T(8,128)(2,1)} fusion(bf16[8,2,64,768]{3,2,1,0:T(8,128)(2,1)} %bitcast.160, pred[8,2]{1,0:T(8,128)(4,1)S(1)} %copy.31), kind=kLoop, calls=%fused_computation.37 | loop fusion | flops 786432 | bytes 3145744 | tf_op jit(solution)/shard_map/jit(_where)/select_n | solution.py:65
  23.1 4.4 %all-to-all-start.1 = ((bf16[8,2,64,768]{3,2,1,0:T(8,128)(2,1)}), bf16[8,2,64,768]{3,2,1,0:T(8,128)(2,1)}, u32[]{:S(2)}, u32[]{:S(2)}) async-start(bf16[8,2,64,768]{3,2,1,0:T(8,128)(2,1)} %broadcast_select_fusion), calls=%async_computation.1 | async-start | bytes 3145728 | tf_op jit(solution)/shard_map/all_to_all | solution.py:66
  27.7 2.0 fusion.77
  30.0 18.5 %all-to-all-done.1 = bf16[8,2,64,768]{3,2,1,0:T(8,128)(2,1)} async-done(((bf16[8,2,64,768]{3,2,1,0:T(8,128)(2,1)}), bf16[8,2,64,768]{3,2,1,0:T(8,128)(2,1)}, u32[]{:S(2)}, u32[]{:S(2)}) %all-to-all-start.1) | async-done | bytes 1572896 | tf_op jit(solution)/shard_map/all_to_all | solution.py:66
  48.6 2.9 %gather_fusion.1 = bf16[8,64,768]{2,1,0:T(8,128)(2,1)} fusion(bf16[16,64,768]{2,1,0:T(8,128)(2,1)} %bitcast.14, s32[1024]{0:T(1024)S(1)} %pad_clamp_fusion), kind=kCustom, calls=%fused_computation.1 | custom fusion | bytes 1572896 | tf_op jit(solution)/shard_map/gather | solution.py:67
  51.4 2.8 %fusion.31 = (u8[64,768]{1,0:T(8,128)(4,1)S(1)}, u8[64,768]{1,0:T(8,128)(4,1)S(1)}, u8[64,768]{1,0:T(8,128)(4,1)S(1)}, f32[8,64,768]{2,1,0:T(8,128)S(1)}) fusion(bf16[8,64,768]{2,1,0:T(8,128)(2,1)} %gather_fusion.1, bf16[768,768]{1,0:T(8,128)(2,1)} %param.15), kind=kOutput, calls=%fused_computation.51 | convolution fusion | flops 611696640 | bytes 3686400 | tf_op jit(solution)/shard_map/dot_general | solution.py:12
  54.3 3.8 %fusion.75 = (f32[8,64]{1,0:T(8,128)S(1)}, f32[8,64,768]{2,1,0:T(8,128)S(1)}) fusion(u8[64,768]{1,0:T(8,128)(4,1)S(1)} %get-tuple-element.38, u8[64,768]{1,0:T(8,128)(4,1)S(1)} %get-tuple-element.39, f32[8,64,768]{2,1,0:T(8,128)S(1)} %get-tuple-element.56, u8[64,768]{1,0:T(8,128)(4,1)S(1)} %get-tuple-element.37), kind=kLoop, calls=%fused_computation.154 | loop fusion | flops 28311040 | bytes 3295232 | tf_op jit(solution)/shard_map/reduce_sum | solution.py:14
  58.7 1.0 maximum_bitcast_fusion
  59.8 0.7 dynamic-slice.1
  60.4 1.6 convolution_reduce_fusion.1
  62.0 1.6 fusion.79
  63.5 0.7 multiply_reduce_fusion.3
  64.9 2.1 fusion.78
  67.3 10.4 %all-gather = bf16[256,768]{1,0:T(8,128)(2,1)S(1)} all-gather(bf16[32,768]{1,0:T(8,128)(2,1)S(1)} %multiply_convert_fusion.2), channel_id=2, replica_groups=mesh['group'=4,'shard'=8] {'shard'}, dimensions={0}, use_global_device_ids=true | all-gather | bytes 442368 | tf_op jit(solution)/shard_map/all_gather | solution.py:49
  77.8 1.4 fusion.20
  79.2 0.9 slice.24
  80.1 50.6 %all-gather.2 = f32[32,10,768]{2,1,0:T(8,128)} all-gather(f32[1,10,768]{2,1,0:T(8,128)S(1)} %fusion.62), channel_id=1, replica_groups=mesh['group'=4,'shard'=8] {'group','shard'}, dimensions={0}, use_global_device_ids=true | all-gather | bytes 1013760 | tf_op jit(solution)/shard_map/all_gather | solution.py:112
  130.8 2.5 reshape.544
  133.3 1.5 fusion.80
  134.8 48.1 %while.2 = (s32[]{:T(128)}, f32[9,8,1920]{2,1,0:T(8,128)}, bf16[9,8,64,768]{3,2,1,0:T(8,128)(2,1)}, bf16[768,1920]{1,0:T(8,128)(2,1)}, s32[]{:T(128)}) while((s32[]{:T(128)}, f32[9,8,1920]{2,1,0:T(8,128)}, bf16[9,8,64,768]{3,2,1,0:T(8,128)(2,1)}, bf16[768,1920]{1,0:T(8,128)(2,1)}, s32[]{:T(128)}) %tuple.40), condition=%wide.region_13.14_spmd, body=%wide.region_11.13_spmd.sunk | while | flops 1511900160 | bytes 3919949 | solution.py:25
  134.8 4.7 %log-plus-one_reduce_fusion.2 = f32[8,1920]{1,0:T(8,128)S(1)} fusion(bf16[768,1920]{1,0:T(8,128)(2,1)} %get-tuple-element.102, bf16[9,8,64,768]{3,2,1,0:T(8,128)(2,1)} %get-tuple-element.101, s32[]{:T(128)S(6)} %copy.45), kind=kOutput, calls=%fused_computation.2.clone.1 | convolution fusion | flops 1511900160 | bytes 3796996 | tf_op jit(solution)/shard_map/while/body/eval_jaxpr/vmap()/dot_general | solution.py:20
  140.2 4.7 %log-plus-one_reduce_fusion.2 = f32[8,1920]{1,0:T(8,128)S(1)} fusion(bf16[768,1920]{1,0:T(8,128)(2,1)} %get-tuple-element.102, bf16[9,8,64,768]{3,2,1,0:T(8,128)(2,1)} %get-tuple-element.101, s32[]{:T(128)S(6)} %copy.45), kind=kOutput, calls=%fused_computation.2.clone.1 | convolution fusion | flops 1511900160 | bytes 3796996 | tf_op jit(solution)/shard_map/while/body/eval_jaxpr/vmap()/dot_general | solution.py:20
  144.9 0.6 bitcast_dynamic-update-slice_fusion.2
  145.5 4.7 %log-plus-one_reduce_fusion.2 = f32[8,1920]{1,0:T(8,128)S(1)} fusion(bf16[768,1920]{1,0:T(8,128)(2,1)} %get-tuple-element.102, bf16[9,8,64,768]{3,2,1,0:T(8,128)(2,1)} %get-tuple-element.101, s32[]{:T(128)S(6)} %copy.45), kind=kOutput, calls=%fused_computation.2.clone.1 | convolution fusion | flops 1511900160 | bytes 3796996 | tf_op jit(solution)/shard_map/while/body/eval_jaxpr/vmap()/dot_general | solution.py:20
  150.3 0.6 bitcast_dynamic-update-slice_fusion.2
  150.9 4.7 %log-plus-one_reduce_fusion.2 = f32[8,1920]{1,0:T(8,128)S(1)} fusion(bf16[768,1920]{1,0:T(8,128)(2,1)} %get-tuple-element.102, bf16[9,8,64,768]{3,2,1,0:T(8,128)(2,1)} %get-tuple-element.101, s32[]{:T(128)S(6)} %copy.45), kind=kOutput, calls=%fused_computation.2.clone.1 | convolution fusion | flops 1511900160 | bytes 3796996 | tf_op jit(solution)/shard_map/while/body/eval_jaxpr/vmap()/dot_general | solution.py:20
  155.6 0.6 bitcast_dynamic-update-slice_fusion.2
  156.2 4.7 %log-plus-one_reduce_fusion.2 = f32[8,1920]{1,0:T(8,128)S(1)} fusion(bf16[768,1920]{1,0:T(8,128)(2,1)} %get-tuple-element.102, bf16[9,8,64,768]{3,2,1,0:T(8,128)(2,1)} %get-tuple-element.101, s32[]{:T(128)S(6)} %copy.45), kind=kOutput, calls=%fused_computation.2.clone.1 | convolution fusion | flops 1511900160 | bytes 3796996 | tf_op jit(solution)/shard_map/while/body/eval_jaxpr/vmap()/dot_general | solution.py:20
  160.9 0.6 bitcast_dynamic-update-slice_fusion.2
  161.6 4.7 %log-plus-one_reduce_fusion.2 = f32[8,1920]{1,0:T(8,128)S(1)} fusion(bf16[768,1920]{1,0:T(8,128)(2,1)} %get-tuple-element.102, bf16[9,8,64,768]{3,2,1,0:T(8,128)(2,1)} %get-tuple-element.101, s32[]{:T(128)S(6)} %copy.45), kind=kOutput, calls=%fused_computation.2.clone.1 | convolution fusion | flops 1511900160 | bytes 3796996 | tf_op jit(solution)/shard_map/while/body/eval_jaxpr/vmap()/dot_general | solution.py:20
  166.3 0.6 bitcast_dynamic-update-slice_fusion.2
  166.9 4.7 %log-plus-one_reduce_fusion.2 = f32[8,1920]{1,0:T(8,128)S(1)} fusion(bf16[768,1920]{1,0:T(8,128)(2,1)} %get-tuple-element.102, bf16[9,8,64,768]{3,2,1,0:T(8,128)(2,1)} %get-tuple-element.101, s32[]{:T(128)S(6)} %copy.45), kind=kOutput, calls=%fused_computation.2.clone.1 | convolution fusion | flops 1511900160 | bytes 3796996 | tf_op jit(solution)/shard_map/while/body/eval_jaxpr/vmap()/dot_general | solution.py:20
  171.6 0.6 bitcast_dynamic-update-slice_fusion.2
  172.3 4.7 %log-plus-one_reduce_fusion.2 = f32[8,1920]{1,0:T(8,128)S(1)} fusion(bf16[768,1920]{1,0:T(8,128)(2,1)} %get-tuple-element.102, bf16[9,8,64,768]{3,2,1,0:T(8,128)(2,1)} %get-tuple-element.101, s32[]{:T(128)S(6)} %copy.45), kind=kOutput, calls=%fused_computation.2.clone.1 | convolution fusion | flops 1511900160 | bytes 3796996 | tf_op jit(solution)/shard_map/while/body/eval_jaxpr/vmap()/dot_general | solution.py:20
  177.6 4.7 %log-plus-one_reduce_fusion.2 = f32[8,1920]{1,0:T(8,128)S(1)} fusion(bf16[768,1920]{1,0:T(8,128)(2,1)} %get-tuple-element.102, bf16[9,8,64,768]{3,2,1,0:T(8,128)(2,1)} %get-tuple-element.101, s32[]{:T(128)S(6)} %copy.45), kind=kOutput, calls=%fused_computation.2.clone.1 | convolution fusion | flops 1511900160 | bytes 3796996 | tf_op jit(solution)/shard_map/while/body/eval_jaxpr/vmap()/dot_general | solution.py:20
  182.9 2.1 reshape_reshape.3
  185.0 2.5 fusion.56
  187.5 12.1 %all-reduce = f32[8,9]{1,0:T(8,128)S(1)} all-reduce(f32[8,9]{1,0:T(8,128)S(1)} %bitcast.165), channel_id=4, replica_groups=mesh['group'=4,'shard'=8] {'shard'}, use_global_device_ids=true, to_apply=%region_14.15.clone | all-reduce | flops 72 | bytes 576
  199.6 0.6 dynamic-slice_multiply_fusion
  200.3 1.4 fusion.74
  201.9 0.7 multiply_multiply_fusion.16
  202.6 0.7 subtract_multiply_fusion
  203.4 44.1 %all-gather.3 = f32[32,10,768]{2,1,0:T(8,128)} all-gather(f32[1,10,768]{2,1,0:T(8,128)S(1)} %maximum_bitcast_fusion.1), channel_id=1, replica_groups=mesh['group'=4,'shard'=8] {'group','shard'}, dimensions={0}, use_global_device_ids=true | all-gather | bytes 1013760 | tf_op jit(solution)/shard_map/all_gather | solution.py:113
  247.5 2.4 reshape.546
  249.9 6.9 %fusion.81 = f32[768,768]{1,0:T(8,128)} fusion(f32[320,768]{1,0:T(8,128)} %reshape.544, f32[320,768]{1,0:T(8,128)} %reshape.546), kind=kOutput, calls=%fused_computation.159 | convolution fusion | flops 2264924160 | bytes 4325376 | tf_op jit(solution)/shard_map/rd,re->de/dot_general | solution.py:29
  (60 shorter events, 4.4 us)
Async XLA Ops:
  7.2 11.4 %copy-start = (bf16[32,64,768]{2,1,0:T(8,128)(2,1)S(1)}, bf16[32,64,768]{2,1,0:T(8,128)(2,1)}, u32[]{:S(2)}) copy-start(bf16[32,64,768]{2,1,0:T(8,128)(2,1)} %param.12) | copy-start | bytes 9437188
  23.1 4.5 %copy-start.5 = (s32[1,8]{1,0:T(1,128)S(1)}, s32[1,8]{1,0:T(1,128)}, u32[]{:S(2)}) copy-start(s32[1,8]{1,0:T(1,128)} %param.13) | copy-start | bytes 100
  23.1 4.5 %copy-start.2 = (bf16[1,64,768]{2,1,0:T(8,128)(2,1)S(1)}, bf16[1,64,768]{2,1,0:T(8,128)(2,1)}, u32[]{:S(2)}) copy-start(bf16[1,64,768]{2,1,0:T(8,128)(2,1)} %param.11) | copy-start | bytes 294916
  23.1 25.4 %all-to-all-start.1 = ((bf16[8,2,64,768]{3,2,1,0:T(8,128)(2,1)}), bf16[8,2,64,768]{3,2,1,0:T(8,128)(2,1)}, u32[]{:S(2)}, u32[]{:S(2)}) async-start(bf16[8,2,64,768]{3,2,1,0:T(8,128)(2,1)} %broadcast_select_fusion), calls=%async_computation.1 | async-start | bytes 3145728 | tf_op jit(solution)/shard_map/all_to_all | solution.py:66
  27.6 107.3 %all-gather.6.cloned.1.call-start = ((), (), s32[]{:S(2)}) async-start(), calls=%async_computation.2 | async-start | bytes 7962624 | tf_op jit(solution)/shard_map/all_gather | solution.py:74
  58.7 1.1 copy-start.6
  58.7 3.3 %copy-start.1 = (bf16[1,32,768]{2,1,0:T(8,128)(2,1)S(1)}, bf16[1,32,768]{2,1,0:T(8,128)(2,1)}, u32[]{:S(2)}) copy-start(bf16[1,32,768]{2,1,0:T(8,128)(2,1)} %param.10) | copy-start | bytes 147460
  64.9 12.8 %copy-start.4 = (bf16[768,1920]{1,0:T(8,128)(2,1)S(1)}, bf16[768,1920]{1,0:T(8,128)(2,1)}, u32[]{:S(2)}) copy-start(bf16[768,1920]{1,0:T(8,128)(2,1)} %param.16) | copy-start | bytes 8847364
  182.9 17.4 %copy-start.3 = (s32[1,8]{1,0:T(1,128)S(1)}, s32[1,8]{1,0:T(1,128)}, u32[]{:S(2)}) copy-start(s32[1,8]{1,0:T(1,128)} %param.14) | copy-start | bytes 100
Sparse Core Ops, SparseCore 0:
  59.9 59.8 all-gather.5
where the time goes:
time: 264 us
  blocking collectives  127 us (48%)
  matrix products  66.2 us (25%)
  local copies, waits for them, and re-layouts  19.4 us (7%)
  waiting for transfers between devices  18.6 us (7%)
  between operations  15.1 us (6%)
  other arithmetic  12.9 us (5%)
  starting transfers between devices  4.46 us (2%)
    all_gather x1, blocking collectives, body(): lax.all_gather(states, ('group', 'shard'), axis=0, tiled=True)  50.6 us
    all_gather x1, blocking collectives, body(): lax.all_gather(factors, ('group', 'shard'), axis=0, tiled=True)  44.1 us
    dot_general x10, matrix products, pool_single(): logits = jnp.dot(sequence, vocab_weight, preferred_element_type=jnp.float32)  43.8 us
    all_to_all x1, waiting for transfers between devices, body(): lax.all_to_all(served, 'shard', split_axis=0, concat_axis=0, tiled=True)  18.5 us
    unnamed x1, blocking collectives  12.1 us
    all_gather x1, blocking collectives, body(): lax.all_gather(query_coded, 'shard', axis=0, tiled=True)  10.4 us
    all_to_all x1, blocking collectives, body(): lax.all_to_all(requests, 'shard', split_axis=0, concat_axis=0, tiled=True)  9.68 us
    dot_general x3, matrix products, encode(): jnp.dot(hidden, transform_weight, preferred_element_type=jnp.float32)  6.94 us
  transfers between devices with their start and end apart: 2, of which 1 were waited for; matrix products, arithmetic and copies ran while one was open for 6% of the time, Pallas kernels for 0%

commit v1 on v0

--- a/solution.py
+++ b/solution.py
@@ -6,6 +6,18 @@
 from jax.sharding import PartitionSpec as P
 
 CAP = 2
+
+
+def gather_by_bits(array, axis, dim):
+    ways, here = (lax.axis_size(axis), lax.axis_index(axis))
+    grown, reach = (array, 1)
+    while reach < ways:
+        theirs = lax.ppermute(grown, axis, [(d, d ^ reach) for d in range(ways)])
+        mine_first = jnp.concatenate([grown, theirs], axis=dim)
+        theirs_first = jnp.concatenate([theirs, grown], axis=dim)
+        grown = jnp.where(here & reach == 0, mine_first, theirs_first)
+        reach = 2 * reach
+    return grown
 
 
 def encode(hidden, transform_weight):
@@ -109,7 +121,7 @@
     dense_grad = add_outer(
         empty,
         (
-            lax.all_gather(states, ("group", "shard"), axis=0, tiled=True),
+            gather_by_bits(states, ("group", "shard"), 0),
             lax.all_gather(factors, ("group", "shard"), axis=0, tiled=True),
         ),
     )

time: 264 us -> 242 us (0.917)
  blocking collectives: 127 us -> 77.5 us
  waiting for transfers between devices: 18.6 us -> 38.7 us
  starting transfers between devices: 4.46 us -> 13.2 us
    all_gather x1 -> x0, blocking collectives: 50.6 us -> none  [body(): lax.all_gather(states, ('group', 'shard'), axis=0, tiled=True)]
    all_gather x1, waiting for transfers between devices: 0.01 us -> 13 us  [body(): lax.all_gather(passages, 'shard', axis=0, tiled=True)]
    ppermute x0 -> x5, starting transfers between devices: none -> 8.77 us  [gather_by_bits(): theirs = lax.ppermute(grown, axis, [(d, d ^ reach) for d in range(ways)])]
    ppermute x0 -> x5, waiting for transfers between devices: none -> 7.1 us  [gather_by_bits(): theirs = lax.ppermute(grown, axis, [(d, d ^ reach) for d in range(ways)])]
    unnamed x18 -> x17, local copies, waits for them, and re-layouts: 5.61 us -> 3.09 us
  transfers between devices with their start and end apart: 2 -> 7, of which waited for: 1 -> 4; matrix products, arithmetic and copies ran while one was open for 6% -> 30% of each run, Pallas kernels for 0% -> 0%
where the time goes in v1:
time: 242 us; the launch traced here: 241 us
  blocking collectives  77.5 us (32%)
  matrix products  66.4 us (27%)
  waiting for transfers between devices  38.7 us (16%)
  local copies, waits for them, and re-layouts  16.9 us (7%)
  between operations  15 us (6%)
  other arithmetic  13.7 us (6%)
  starting transfers between devices  13.2 us (5%)
    all_gather x1, blocking collectives, body(): lax.all_gather(factors, ('group', 'shard'), axis=0, tiled=True)  46 us
    dot_general x10, matrix products, pool_single(): logits = jnp.dot(sequence, vocab_weight, preferred_element_type=jnp.float32)  43.7 us
    all_to_all x1, waiting for transfers between devices, body(): lax.all_to_all(served, 'shard', split_axis=0, concat_axis=0, tiled=True)  18.5 us
    unnamed x1, blocking collectives  13.1 us
    all_gather x1, waiting for transfers between devices, body(): lax.all_gather(passages, 'shard', axis=0, tiled=True)  13 us
    all_to_all x1, blocking collectives, body(): lax.all_to_all(requests, 'shard', split_axis=0, concat_axis=0, tiled=True)  9.68 us
    all_gather x1, blocking collectives, body(): lax.all_gather(query_coded, 'shard', axis=0, tiled=True)  8.79 us
    ppermute x5, starting transfers between devices, gather_by_bits(): theirs = lax.ppermute(grown, axis, [(d, d ^ reach) for d in range(ways)])  8.77 us
  transfers between devices with their start and end apart: 7, of which 4 were waited for; matrix products, arithmetic and copies ran while one was open for 30% of the time, Pallas kernels for 0%

profile of v1, /device:TPU:0, one launch (start us, length us, event | category | flops | bytes accessed | tf_op | source)
XLA Modules:
  0.0 241.5 jit_solution(10235218359508459953)
XLA Ops:
  7.2 0.8 and_select_fusion.2
  8.6 9.7 %all_to_all.11 = s32[8,1,2]{2,1,0:T(1,128)S(1)} all-to-all(s32[8,1,2]{2,1,0:T(1,128)S(1)} %copy.29), channel_id=1, replica_groups=mesh['group'=4,'shard'=8] {'shard'}, dimensions={0} | all-to-all | bytes 128 | tf_op jit(solution)/shard_map/all_to_all | solution.py:74
  18.6 1.8 gather_fusion
  20.4 2.7 %broadcast_select_fusion = bf16[8,2,64,768]{3,2,1,0:T(8,128)(2,1)} fusion(bf16[8,2,64,768]{3,2,1,0:T(8,128)(2,1)} %bitcast.154, pred[8,2]{1,0:T(8,128)(4,1)S(1)} %copy.31), kind=kLoop, calls=%fused_computation.37 | loop fusion | flops 786432 | bytes 3145744 | tf_op jit(solution)/shard_map/jit(_where)/select_n | solution.py:77
  23.1 4.4 %all-to-all-start.1 = ((bf16[8,2,64,768]{3,2,1,0:T(8,128)(2,1)}), bf16[8,2,64,768]{3,2,1,0:T(8,128)(2,1)}, u32[]{:S(2)}, u32[]{:S(2)}) async-start(bf16[8,2,64,768]{3,2,1,0:T(8,128)(2,1)} %broadcast_select_fusion), calls=%async_computation.1 | async-start | bytes 3145728 | tf_op jit(solution)/shard_map/all_to_all | solution.py:78
  27.7 2.0 fusion.84
  30.0 18.5 %all-to-all-done.1 = bf16[8,2,64,768]{3,2,1,0:T(8,128)(2,1)} async-done(((bf16[8,2,64,768]{3,2,1,0:T(8,128)(2,1)}), bf16[8,2,64,768]{3,2,1,0:T(8,128)(2,1)}, u32[]{:S(2)}, u32[]{:S(2)}) %all-to-all-start.1) | async-done | bytes 1572896 | tf_op jit(solution)/shard_map/all_to_all | solution.py:78
  48.6 2.9 %gather_fusion.1 = bf16[8,64,768]{2,1,0:T(8,128)(2,1)} fusion(bf16[16,64,768]{2,1,0:T(8,128)(2,1)} %bitcast.14, s32[1024]{0:T(1024)S(1)} %pad_clamp_fusion), kind=kCustom, calls=%fused_computation.1 | custom fusion | bytes 1572896 | tf_op jit(solution)/shard_map/gather | solution.py:79
  51.4 2.8 %fusion.38 = (u8[64,768]{1,0:T(8,128)(4,1)S(1)}, u8[64,768]{1,0:T(8,128)(4,1)S(1)}, u8[64,768]{1,0:T(8,128)(4,1)S(1)}, f32[8,64,768]{2,1,0:T(8,128)S(1)}) fusion(bf16[8,64,768]{2,1,0:T(8,128)(2,1)} %gather_fusion.1, bf16[768,768]{1,0:T(8,128)(2,1)} %param.15), kind=kOutput, calls=%fused_computation.60 | convolution fusion | flops 611696640 | bytes 3686400 | tf_op jit(solution)/shard_map/dot_general | solution.py:24
  54.3 3.8 %fusion.82 = (f32[8,64]{1,0:T(8,128)S(1)}, f32[8,64,768]{2,1,0:T(8,128)S(1)}) fusion(u8[64,768]{1,0:T(8,128)(4,1)S(1)} %get-tuple-element.38, u8[64,768]{1,0:T(8,128)(4,1)S(1)} %get-tuple-element.39, f32[8,64,768]{2,1,0:T(8,128)S(1)} %get-tuple-element.56, u8[64,768]{1,0:T(8,128)(4,1)S(1)} %get-tuple-element.37), kind=kLoop, calls=%fused_computation.166 | loop fusion | flops 28311040 | bytes 3295232 | tf_op jit(solution)/shard_map/reduce_sum | solution.py:26
  58.7 1.0 maximum_bitcast_fusion
  59.7 2.0 fusion.85
  62.0 8.8 %all-gather = bf16[256,768]{1,0:T(8,128)(2,1)S(1)} all-gather(bf16[32,768]{1,0:T(8,128)(2,1)S(1)} %multiply_convert_fusion.2), channel_id=2, replica_groups=mesh['group'=4,'shard'=8] {'shard'}, dimensions={0}, use_global_device_ids=true | all-gather | bytes 442368 | tf_op jit(solution)/shard_map/all_gather | solution.py:61
  70.8 0.9 slice.24
  72.2 1.4 fusion.20
  73.7 2.3 collective-permute-start.1
  75.9 1.6 fusion.86
  77.5 3.0 %collective-permute-done.1 = f32[20,768]{1,0:T(8,128)S(1)} collective-permute-done((f32[20,768]{1,0:T(8,128)S(1)}, f32[20,768]{1,0:T(8,128)S(1)}, u32[]{:S(2)}, u32[]{:S(2)}) %collective-permute-start.1) | collective-permute-done | bytes 61472 | tf_op jit(solution)/shard_map/ppermute | solution.py:15
  80.5 1.9 collective-permute-start.2
  82.4 1.6 convolution_reduce_fusion.1
  84.0 0.6 dynamic-slice.1
  85.9 1.6 collective-permute-start.3
  87.5 1.5 fusion.87
  89.0 4.1 %collective-permute-done.3 = f32[80,768]{1,0:T(8,128)S(1)} collective-permute-done((f32[80,768]{1,0:T(8,128)S(1)}, f32[80,768]{1,0:T(8,128)S(1)}, u32[]{:S(2)}, u32[]{:S(2)}) %collective-permute-start.3) | collective-permute-done | bytes 245792 | tf_op jit(solution)/shard_map/ppermute | solution.py:15
  93.1 0.8 maximum_select_fusion.2
  94.0 2.6 %collective-permute-start.4 = (f32[160,768]{1,0:T(8,128)}, f32[160,768]{1,0:T(8,128)}, u32[]{:S(2)}, u32[]{:S(2)}) collective-permute-start(f32[160,768]{1,0:T(8,128)} %maximum_select_fusion.2), channel_id=1, source_target_pairs={{0,16},{1,17},{2,18},{3,19},{4,20},{5,21},{6,22},{7,23},{8,24},{9,... | collective-permute-start | bytes 1474568 | tf_op jit(solution)/shard_map/ppermute | solution.py:15
  96.6 13.0 %all-gather.5.cloned.1.call-done = bf16[1,72,64,768]{3,2,0,1:T(8,128)(2,1)} async-done(((bf16[1,9,64,768]{3,2,0,1:T(8,128)(2,1)}), bf16[1,72,64,768]{3,2,0,1:T(8,128)(2,1)}) %all-gather.5.cloned.1.call-update) | async-done | bytes 7077904 | tf_op jit(solution)/shard_map/all_gather | solution.py:86
  109.6 48.1 %while.2 = (s32[]{:T(128)}, f32[9,8,1920]{2,1,0:T(8,128)}, bf16[9,8,64,768]{3,2,1,0:T(8,128)(2,1)}, bf16[768,1920]{1,0:T(8,128)(2,1)}, s32[]{:T(128)}) while((s32[]{:T(128)}, f32[9,8,1920]{2,1,0:T(8,128)}, bf16[9,8,64,768]{3,2,1,0:T(8,128)(2,1)}, bf16[768,1920]{1,0:T(8,128)(2,1)}, s32[]{:T(128)}) %tuple.40), condition=%wide.region_13.14_spmd, body=%wide.region_11.13_spmd.sunk | while | flops 1511900160 | bytes 3919949 | solution.py:37
  109.6 4.7 %log-plus-one_reduce_fusion.2 = f32[8,1920]{1,0:T(8,128)S(1)} fusion(bf16[768,1920]{1,0:T(8,128)(2,1)} %get-tuple-element.102, bf16[9,8,64,768]{3,2,1,0:T(8,128)(2,1)} %get-tuple-element.101, s32[]{:T(128)S(6)} %copy.45), kind=kOutput, calls=%fused_computation.2.clone.1 | convolution fusion | flops 1511900160 | bytes 3796996 | tf_op jit(solution)/shard_map/while/body/eval_jaxpr/vmap()/dot_general | solution.py:32
  114.9 4.7 %log-plus-one_reduce_fusion.2 = f32[8,1920]{1,0:T(8,128)S(1)} fusion(bf16[768,1920]{1,0:T(8,128)(2,1)} %get-tuple-element.102, bf16[9,8,64,768]{3,2,1,0:T(8,128)(2,1)} %get-tuple-element.101, s32[]{:T(128)S(6)} %copy.45), kind=kOutput, calls=%fused_computation.2.clone.1 | convolution fusion | flops 1511900160 | bytes 3796996 | tf_op jit(solution)/shard_map/while/body/eval_jaxpr/vmap()/dot_general | solution.py:32
  120.3 4.7 %log-plus-one_reduce_fusion.2 = f32[8,1920]{1,0:T(8,128)S(1)} fusion(bf16[768,1920]{1,0:T(8,128)(2,1)} %get-tuple-element.102, bf16[9,8,64,768]{3,2,1,0:T(8,128)(2,1)} %get-tuple-element.101, s32[]{:T(128)S(6)} %copy.45), kind=kOutput, calls=%fused_computation.2.clone.1 | convolution fusion | flops 1511900160 | bytes 3796996 | tf_op jit(solution)/shard_map/while/body/eval_jaxpr/vmap()/dot_general | solution.py:32
  125.6 4.7 %log-plus-one_reduce_fusion.2 = f32[8,1920]{1,0:T(8,128)S(1)} fusion(bf16[768,1920]{1,0:T(8,128)(2,1)} %get-tuple-element.102, bf16[9,8,64,768]{3,2,1,0:T(8,128)(2,1)} %get-tuple-element.101, s32[]{:T(128)S(6)} %copy.45), kind=kOutput, calls=%fused_computation.2.clone.1 | convolution fusion | flops 1511900160 | bytes 3796996 | tf_op jit(solution)/shard_map/while/body/eval_jaxpr/vmap()/dot_general | solution.py:32
  130.3 0.6 bitcast_dynamic-update-slice_fusion.2
  130.9 4.7 %log-plus-one_reduce_fusion.2 = f32[8,1920]{1,0:T(8,128)S(1)} fusion(bf16[768,1920]{1,0:T(8,128)(2,1)} %get-tuple-element.102, bf16[9,8,64,768]{3,2,1,0:T(8,128)(2,1)} %get-tuple-element.101, s32[]{:T(128)S(6)} %copy.45), kind=kOutput, calls=%fused_computation.2.clone.1 | convolution fusion | flops 1511900160 | bytes 3796996 | tf_op jit(solution)/shard_map/while/body/eval_jaxpr/vmap()/dot_general | solution.py:32
  135.7 0.6 bitcast_dynamic-update-slice_fusion.2
  136.3 4.7 %log-plus-one_reduce_fusion.2 = f32[8,1920]{1,0:T(8,128)S(1)} fusion(bf16[768,1920]{1,0:T(8,128)(2,1)} %get-tuple-element.102, bf16[9,8,64,768]{3,2,1,0:T(8,128)(2,1)} %get-tuple-element.101, s32[]{:T(128)S(6)} %copy.45), kind=kOutput, calls=%fused_computation.2.clone.1 | convolution fusion | flops 1511900160 | bytes 3796996 | tf_op jit(solution)/shard_map/while/body/eval_jaxpr/vmap()/dot_general | solution.py:32
  141.6 4.7 %log-plus-one_reduce_fusion.2 = f32[8,1920]{1,0:T(8,128)S(1)} fusion(bf16[768,1920]{1,0:T(8,128)(2,1)} %get-tuple-element.102, bf16[9,8,64,768]{3,2,1,0:T(8,128)(2,1)} %get-tuple-element.101, s32[]{:T(128)S(6)} %copy.45), kind=kOutput, calls=%fused_computation.2.clone.1 | convolution fusion | flops 1511900160 | bytes 3796996 | tf_op jit(solution)/shard_map/while/body/eval_jaxpr/vmap()/dot_general | solution.py:32
  147.0 4.7 %log-plus-one_reduce_fusion.2 = f32[8,1920]{1,0:T(8,128)S(1)} fusion(bf16[768,1920]{1,0:T(8,128)(2,1)} %get-tuple-element.102, bf16[9,8,64,768]{3,2,1,0:T(8,128)(2,1)} %get-tuple-element.101, s32[]{:T(128)S(6)} %copy.45), kind=kOutput, calls=%fused_computation.2.clone.1 | convolution fusion | flops 1511900160 | bytes 3796996 | tf_op jit(solution)/shard_map/while/body/eval_jaxpr/vmap()/dot_general | solution.py:32
  152.3 4.7 %log-plus-one_reduce_fusion.2 = f32[8,1920]{1,0:T(8,128)S(1)} fusion(bf16[768,1920]{1,0:T(8,128)(2,1)} %get-tuple-element.102, bf16[9,8,64,768]{3,2,1,0:T(8,128)(2,1)} %get-tuple-element.101, s32[]{:T(128)S(6)} %copy.45), kind=kOutput, calls=%fused_computation.2.clone.1 | convolution fusion | flops 1511900160 | bytes 3796996 | tf_op jit(solution)/shard_map/while/body/eval_jaxpr/vmap()/dot_general | solution.py:32
  157.7 2.1 reshape_reshape.3
  159.8 2.5 %fusion.63 = f32[8,1,9]{2,1,0:T(1,128)S(1)} fusion(f32[8,9,1920]{2,1,0:T(8,128)} %reshape_reshape.3, f32[8,1920,1]{1,0,2:T(8,128)S(1)} %bitcast.158), kind=kOutput, calls=%fused_computation.108 | convolution fusion | flops 1658880 | bytes 614688 | tf_op jit(solution)/shard_map/qv,qjv->qj/dot_general | solution.py:88
  162.2 13.1 %all-reduce = f32[8,9]{1,0:T(8,128)S(1)} all-reduce(f32[8,9]{1,0:T(8,128)S(1)} %bitcast.159), channel_id=4, replica_groups=mesh['group'=4,'shard'=8] {'shard'}, use_global_device_ids=true, to_apply=%region_14.15.clone | all-reduce | flops 72 | bytes 576
  176.0 1.4 fusion.81
  177.6 0.7 multiply_multiply_fusion.16
  178.3 0.7 subtract_multiply_fusion
  179.1 46.0 %all-gather.2 = f32[32,10,768]{2,1,0:T(8,128)} all-gather(f32[1,10,768]{2,1,0:T(8,128)S(1)} %maximum_bitcast_fusion.1), channel_id=1, replica_groups=mesh['group'=4,'shard'=8] {'group','shard'}, dimensions={0}, use_global_device_ids=true | all-gather | bytes 1013760 | tf_op jit(solution)/shard_map/all_gather | solution.py:125
  225.0 2.4 reshape.544
  227.4 7.2 %fusion.29 = f32[768,768]{1,0:T(8,128)} fusion(f32[320,768]{1,0:T(8,128)} %reshape.544, f32[160,768]{1,0:T(8,128)} %collective-permute-done.4, f32[160,768]{1,0:T(8,128)} %maximum_select_fusion.2, pred[]{:T(512)S(6)} %eq.58), kind=kOutput, calls=%fused_computation.49 | convolution fusion | flops 2265661440 | bytes 4325377 | tf_op jit(solution)/shard_map/rd,re->de/dot_general | solution.py:41
  (72 shorter events, 8.6 us)
Async XLA Ops:
  7.2 11.4 %copy-start = (bf16[32,64,768]{2,1,0:T(8,128)(2,1)S(1)}, bf16[32,64,768]{2,1,0:T(8,128)(2,1)}, u32[]{:S(2)}) copy-start(bf16[32,64,768]{2,1,0:T(8,128)(2,1)} %param.12) | copy-start | bytes 9437188
  23.1 4.5 %copy-start.5 = (s32[1,8]{1,0:T(1,128)S(1)}, s32[1,8]{1,0:T(1,128)}, u32[]{:S(2)}) copy-start(s32[1,8]{1,0:T(1,128)} %param.13) | copy-start | bytes 100
  23.1 4.5 %copy-start.2 = (bf16[1,64,768]{2,1,0:T(8,128)(2,1)S(1)}, bf16[1,64,768]{2,1,0:T(8,128)(2,1)}, u32[]{:S(2)}) copy-start(bf16[1,64,768]{2,1,0:T(8,128)(2,1)} %param.11) | copy-start | bytes 294916
  23.1 25.4 %all-to-all-start.1 = ((bf16[8,2,64,768]{3,2,1,0:T(8,128)(2,1)}), bf16[8,2,64,768]{3,2,1,0:T(8,128)(2,1)}, u32[]{:S(2)}, u32[]{:S(2)}) async-start(bf16[8,2,64,768]{3,2,1,0:T(8,128)(2,1)} %broadcast_select_fusion), calls=%async_computation.1 | async-start | bytes 3145728 | tf_op jit(solution)/shard_map/all_to_all | solution.py:78
  27.6 82.0 %all-gather.5.cloned.1.call-start = ((), (), s32[]{:S(2)}) async-start(), calls=%async_computation.2 | async-start | bytes 7962624 | tf_op jit(solution)/shard_map/all_gather | solution.py:86
  58.7 1.0 copy-start.1
  59.7 12.5 %copy-start.4 = (bf16[768,1920]{1,0:T(8,128)(2,1)S(1)}, bf16[768,1920]{1,0:T(8,128)(2,1)}, u32[]{:S(2)}) copy-start(bf16[768,1920]{1,0:T(8,128)(2,1)} %param.16) | copy-start | bytes 8847364
  71.8 1.9 collective-permute-start
  73.6 10.4 %copy-start.6 = (u32[32]{0:T(128)S(1)}, u32[32]{0:T(128)}, u32[]{:S(2)}) copy-start(u32[32]{0:T(128)} %constant.46) | copy-start | bytes 388
  73.7 6.8 %collective-permute-start.1 = (f32[20,768]{1,0:T(8,128)S(1)}, f32[20,768]{1,0:T(8,128)S(1)}, u32[]{:S(2)}, u32[]{:S(2)}) collective-permute-start(f32[20,768]{1,0:T(8,128)S(1)} %maximum_select_fusion.5), channel_id=1, source_target_pairs={{0,2},{1,3},{2,0},{3,1},{4,6},{5,7},{6,4},{7,5},{8,10},{9,11},{10,... | collective-permute-start | bytes 184328 | tf_op jit(solution)/shard_map/ppermute | solution.py:15
  80.5 5.3 %collective-permute-start.2 = (f32[40,768]{1,0:T(8,128)S(1)}, f32[40,768]{1,0:T(8,128)S(1)}, u32[]{:S(2)}, u32[]{:S(2)}) collective-permute-start(f32[40,768]{1,0:T(8,128)S(1)} %maximum_select_fusion.4), channel_id=1, source_target_pairs={{0,4},{1,5},{2,6},{3,7},{4,0},{5,1},{6,2},{7,3},{8,12},{9,13},{10,... | collective-permute-start | bytes 368648 | tf_op jit(solution)/shard_map/ppermute | solution.py:15
  85.9 7.3 %collective-permute-start.3 = (f32[80,768]{1,0:T(8,128)S(1)}, f32[80,768]{1,0:T(8,128)S(1)}, u32[]{:S(2)}, u32[]{:S(2)}) collective-permute-start(f32[80,768]{1,0:T(8,128)S(1)} %maximum_select_fusion.3), channel_id=1, source_target_pairs={{0,8},{1,9},{2,10},{3,11},{4,12},{5,13},{6,14},{7,15},{8,0},{9,1},... | collective-permute-start | bytes 737288 | tf_op jit(solution)/shard_map/ppermute | solution.py:15
  94.0 133.5 %collective-permute-start.4 = (f32[160,768]{1,0:T(8,128)}, f32[160,768]{1,0:T(8,128)}, u32[]{:S(2)}, u32[]{:S(2)}) collective-permute-start(f32[160,768]{1,0:T(8,128)} %maximum_select_fusion.2), channel_id=1, source_target_pairs={{0,16},{1,17},{2,18},{3,19},{4,20},{5,21},{6,22},{7,23},{8,24},{9,... | collective-permute-start | bytes 1474568 | tf_op jit(solution)/shard_map/ppermute | solution.py:15
  157.7 18.3 %copy-start.3 = (s32[1,8]{1,0:T(1,128)S(1)}, s32[1,8]{1,0:T(1,128)}, u32[]{:S(2)}) copy-start(s32[1,8]{1,0:T(1,128)} %param.14) | copy-start | bytes 100
Sparse Core Ops, SparseCore 0:
  59.8 49.6 all-gather.4
